TPU v7x, 256 devices: a whole 4x4x8 slice. The times are simulated.
256 devices in a mesh: req: 32 (over y, x, core), head: 8 (over z).
Axes of the slice: x: 4, y: 4, z: 8, core: 2. Of those that a mesh axis runs over, the one named last changes fastest.
Arguments:
- tokens: bfloat16 [4096, 1536], P(('req', 'head')), may hold values from -6 to 6
- pre_gain: float32 [1536], replicated, may hold values from 0.1 to 1.9
- inner_weight: bfloat16 [1536, 2, 3072], P(None, None, 'head')
- shared_weight: bfloat16 [1536, 304], replicated, may hold values from -0.15625 to 0.15625
- conv_inner: float32 [4, 3072], P(None, 'head'), may hold values from -0.5 to 0.5
- conv_inner_bias: float32 [3072], P('head'), may hold values from -0.5 to 0.5
- conv_shared: float32 [4, 256], replicated, may hold values from -0.5 to 0.5
- conv_shared_bias: float32 [256], replicated, may hold values from -0.5 to 0.5
- step_bias: float32 [48], P('head'), may hold values from -4 to 0
- decay_log: float32 [48], P('head'), may hold values from 0 to 2.77
- skip_gain: float32 [48], P('head'), may hold values from 0.5 to 1.5
- gate_gain: float32 [3072], P('head'), may hold values from 0.1 to 1.9
- out_weight: bfloat16 [3072, 1536], P('head'), may hold values from -0.109375 to 0.109375
- states: bfloat16 [1024, 48, 64, 128], P('req', 'head'), may hold values from -1.1953125 to 1.1953125
- edge_inner: bfloat16 [1024, 3, 3072], P('req', None, 'head'), may hold values from -6 to 6
- edge_shared: bfloat16 [1024, 3, 256], P('req'), may hold values from -6 to 6
- counts: int32 [1024], P('req'), may hold values from 1 to 4, as said below
- mig_ids: int32 [32], replicated, may hold values from 0 to 1023, as said below
- mig_dest: int32 [32], replicated, may hold values from 0 to 1023, as said below
- reorder: int32 [1024], replicated, may hold values from 0 to 1023, as said below
Outputs:
- hidden_out: bfloat16 [4096, 1536], P(('req', 'head'))
- states_out: bfloat16 [1024, 48, 64, 128], P('req', 'head')
- edge_inner_out: bfloat16 [1024, 3, 3072], P('req', None, 'head')
- edge_shared_out: bfloat16 [1024, 3, 256], P('req')
Inputs may be any that keep to these rules, and one draw needn't show every extreme that they name: counts: each slot's token rows are r * 4 to r * 4 + 3 of tokens; the first counts[r] of them are real. mig_ids: distinct old slots listed by owner: entry i is one of the slots i * 32 to (i + 1) * 32 - 1, those held by index i of req. mig_dest: a reordering of the slots in mig_ids. reorder: a permutation of all slots. The 32 new slots j with j // 32 = d take at most 1 values reorder[j] of any one block of 32 slots, and exactly 1 of some block.
All inputs are finite; a program needn't handle non-finite values.
Results may differ from a plain program's by a relative error of at most 0.013.
Values may be sent and summed in bfloat16 or wider, within the bound.
A program may use at most 128 MiB of HBM per device.

v0:
```python
import jax
import jax.numpy as jnp
from jax import lax
from jax.sharding import PartitionSpec as P

EPS = 1e-05
HIGH = lax.Precision.HIGHEST


def depthwise(edge, fresh, weight, offset_bias):
    sequence = jnp.concatenate([edge, fresh], axis=1).astype(jnp.float32)
    window = fresh.shape[1]
    summed = sequence[:, 0:window] * weight[0]
    for offset in range(1, weight.shape[0]):
        summed = summed + sequence[:, offset : offset + window] * weight[offset]
    return jax.nn.silu(summed + offset_bias)


def new_edge(edge, fresh, counts):
    sequence = jnp.concatenate([edge, fresh], axis=1)
    keep_rows = edge.shape[1]
    result = edge
    for length in range(1, fresh.shape[1] + 1):
        result = jnp.where(
            (counts == length)[:, None, None], sequence[:, length : length + keep_rows], result
        )
    return result


def rank_rows(partner, position, capacity):
    matching = partner[:, None] == partner[None, :]
    earlier = position[None, :] < position[:, None]
    ranking = jnp.sum(jnp.logical_and(matching, earlier), axis=1)
    return partner * capacity + ranking


def route_rows(anchor, first_slot, slot_count, all_slots, capacity):
    inverse = jnp.zeros(all_slots.shape, jnp.int32).at[anchor].set(all_slots)
    targets = lax.dynamic_slice_in_dim(inverse, first_slot, slot_count)
    send_rows = rank_rows(targets // slot_count, targets % slot_count, capacity)
    sources = lax.dynamic_slice_in_dim(anchor, first_slot, slot_count)
    recv_rows = rank_rows(sources // slot_count, jnp.arange(slot_count, dtype=jnp.int32), capacity)
    return (send_rows, recv_rows)


def migrate(item, mig_dest, slot_count, groups, device):
    length = item.shape[0]
    piece = -(-length // groups)
    padded = jnp.pad(item, (0, piece * groups - length)).reshape(groups, piece)
    first = lax.all_to_all(padded, "req", 0, 0, tiled=True)
    dest_dev = mig_dest // slot_count
    order = jnp.zeros((groups,), jnp.int32).at[dest_dev].set(jnp.arange(groups, dtype=jnp.int32))
    second = lax.all_to_all(first[order], "req", 0, 0, tiled=True)
    arrived = second.reshape(-1)[:length]
    target_local = mig_dest[order[device]] - device * slot_count
    return (arrived, target_local)


def local(
    tokens,
    pre_gain,
    inner_weight,
    shared_weight,
    conv_inner,
    conv_inner_bias,
    conv_shared,
    conv_shared_bias,
    step_bias,
    decay_log,
    skip_gain,
    gate_gain,
    out_weight,
    states,
    edge_inner,
    edge_shared,
    counts,
    mig_ids,
    mig_dest,
    reorder,
):
    slot_count, heads_here, head_dim, state_dim = states.shape
    inner_here = heads_here * head_dim
    lanes = state_dim
    groups = lax.axis_size("req")
    device = lax.axis_index("req")
    first_slot = device * slot_count
    stride = (slot_count + groups - 1) // groups
    all_slots = jnp.arange(slot_count * groups, dtype=jnp.int32)
    rows_in = tokens.astype(jnp.float32)
    normed = (
        rows_in * lax.rsqrt(jnp.mean(rows_in * rows_in, axis=-1, keepdims=True) + EPS) * pre_gain
    ).astype(jnp.bfloat16)
    inner_flat = inner_weight.reshape(inner_weight.shape[0], 2 * inner_here)
    piece_rows = lax.all_gather(normed, "head", axis=0, tiled=True)
    inner_rows = jnp.dot(piece_rows, inner_flat, preferred_element_type=jnp.float32).astype(
        jnp.bfloat16
    )
    shared_rows = jnp.dot(piece_rows, shared_weight, preferred_element_type=jnp.float32).astype(
        jnp.bfloat16
    )
    state_rows = heads_here * head_dim * state_dim // lanes
    inner_edge_rows = edge_inner.shape[1] * edge_inner.shape[2] // lanes
    shared_edge_rows = edge_shared.shape[1] * edge_shared.shape[2] // lanes
    packed = jnp.concatenate(
        [
            states.reshape(slot_count, state_rows, lanes),
            edge_inner.reshape(slot_count, inner_edge_rows, lanes),
            edge_shared.reshape(slot_count, shared_edge_rows, lanes),
        ],
        axis=1,
    )
    row_total = packed.shape[1]
    moving = mig_ids.shape[0] // groups
    own_id = mig_ids[device * moving]
    mig_local = own_id - first_slot
    item = lax.dynamic_index_in_dim(packed, mig_local, 0, keepdims=False).reshape(-1)
    arrived, target_local = migrate(item, mig_dest, slot_count, groups, device)
    arrived = arrived.reshape(row_total, lanes)
    send_rows, recv_rows = route_rows(reorder, first_slot, slot_count, all_slots, stride)
    buffer_rows = groups * stride
    send_idx = (
        jnp.zeros((buffer_rows,), jnp.int32)
        .at[send_rows]
        .set(jnp.arange(slot_count, dtype=jnp.int32))
    )
    send_buf = jnp.where((send_idx == target_local)[:, None, None], arrived[None], packed[send_idx])
    received = lax.all_to_all(send_buf, "req", 0, 0, tiled=True)
    moved = received[recv_rows]
    moved_states = moved[:, :state_rows].reshape(slot_count, heads_here, head_dim, state_dim)
    moved_inner = moved[:, state_rows : state_rows + inner_edge_rows].reshape(edge_inner.shape)
    moved_shared = moved[:, state_rows + inner_edge_rows :].reshape(edge_shared.shape)
    window = inner_rows.shape[0] // slot_count
    inner_rows = inner_rows.reshape(slot_count, window, 2 * inner_here)
    shared_rows = shared_rows.reshape(slot_count, window, shared_rows.shape[1])
    gate_part = inner_rows[:, :, :inner_here]
    value_part = inner_rows[:, :, inner_here:]
    fresh_shared = shared_rows[:, :, : 2 * state_dim]
    head_index = lax.axis_index("head")
    step_raw = lax.dynamic_slice_in_dim(
        shared_rows[:, :, 2 * state_dim :], head_index * heads_here, heads_here, axis=2
    )
    edge_inner_out = new_edge(moved_inner, value_part, counts)
    edge_shared_out = new_edge(moved_shared, fresh_shared, counts)
    mixed_inner = depthwise(moved_inner, value_part, conv_inner, conv_inner_bias)
    mixed_shared = depthwise(moved_shared, fresh_shared, conv_shared, conv_shared_bias)
    valid = jnp.arange(window)[None, :] < counts[:, None]
    step_size = jax.nn.softplus(step_raw.astype(jnp.float32) + step_bias)
    step_size = jnp.where(valid[:, :, None], step_size, 0.0)
    decay = -jnp.exp(decay_log)
    inputs = mixed_inner.reshape(slot_count, window, heads_here, head_dim)
    entries = mixed_shared[:, :, :state_dim]
    readouts = mixed_shared[:, :, state_dim:]
    factor = jnp.exp(step_size * decay)
    cum = [factor[:, 0]]
    for t in range(1, window):
        cum.append(cum[-1] * factor[:, t])
    cumulative = jnp.stack(cum, axis=1)
    span = {}
    for t in range(window):
        span[t, t] = jnp.ones_like(factor[:, 0])
        for s in range(t - 1, -1, -1):
            span[t, s] = span[t, s + 1] * factor[:, s + 1]
    held = moved_states.astype(jnp.float32)
    from_state = jnp.einsum("rhpn,rtn->rthp", held, readouts, precision=HIGH)
    overlap = jnp.einsum("rtn,rsn->rts", readouts, entries, precision=HIGH)
    weighted = step_size[:, :, :, None] * inputs
    produced = []
    for t in range(window):
        acc = cumulative[:, t, :, None] * from_state[:, t]
        for s in range(t + 1):
            coef = span[t, s] * overlap[:, t, s, None]
            acc = acc + coef[:, :, None] * weighted[:, s]
        produced.append(acc + skip_gain[None, :, None] * inputs[:, t])
    outputs = jnp.stack(produced, axis=1)
    last = window - 1
    pushed = jnp.stack([span[last, s] for s in range(window)], axis=1)[:, :, :, None] * weighted
    update = jnp.einsum("rshp,rsn->rhpn", pushed, entries, precision=HIGH)
    final = cumulative[:, last, :, None, None] * held + update
    states_out = final.astype(jnp.bfloat16)
    outputs = outputs.reshape(slot_count, window, inner_here)
    gated = outputs * jax.nn.silu(gate_part.astype(jnp.float32))
    square_part = jnp.sum(gated * gated, axis=-1).reshape(slot_count * window, 1)
    pre_scaled = (
        jnp.where(valid[:, :, None], gated * gate_gain, 0.0)
        .astype(jnp.bfloat16)
        .reshape(slot_count * window, inner_here)
    )
    partial = jnp.dot(pre_scaled, out_weight, preferred_element_type=jnp.float32)
    extra = jnp.broadcast_to(square_part, (partial.shape[0], 128))
    combined = jnp.concatenate([partial, extra], axis=1)
    reduced = lax.psum_scatter(combined, "head", scatter_dimension=0, tiled=True)
    full_inner = inner_here * lax.axis_size("head")
    scale = lax.rsqrt(reduced[:, -1:] / full_inner + EPS)
    hidden_out = (rows_in + reduced[:, : partial.shape[1]] * scale).astype(jnp.bfloat16)
    return (hidden_out, states_out, edge_inner_out, edge_shared_out)


def solution(mesh):
    placed = (
        P(("req", "head"), None),
        P(),
        P(None, None, "head"),
        P(),
        P(None, "head"),
        P("head"),
        P(),
        P(),
        P("head"),
        P("head"),
        P("head"),
        P("head"),
        P("head", None),
        P("req", "head", None, None),
        P("req", None, "head"),
        P("req", None, None),
        P("req"),
        P(),
        P(),
        P(),
    )
    return jax.shard_map(
        local,
        mesh=mesh,
        in_specs=placed,
        out_specs=(
            P(("req", "head"), None),
            P("req", "head", None, None),
            P("req", None, "head"),
            P("req", None, None),
        ),
        check_vma=False,
    )
```

profile of v0, /device:TPU:6, one launch (start us, length us, event | category | flops | bytes accessed | tf_op | source)
XLA Modules:
  0.0 188.7 jit_solution(13441082247929192009)
XLA Ops:
  7.2 1.3 dynamic_slice.26
  9.2 0.8 copy.235
  10.1 0.9 copy.234
  11.1 2.3 %pad_maximum_fusion = bf16[32,399,128]{2,1,0:T(8,128)(2,1)S(1)} fusion(bf16[32,6,128]{2,1,0:T(8,128)(2,1)S(1)} %reshape.332, bf16[32,9,128]{2,1,0:T(8,128)(2,1)S(1)} %reshape.331, bf16[32,384,128]{2,1,0:T(8,128)(2,1)} %bitcast.73), kind=kLoop, calls=%fused_computation.7 | loop fusion | flops 9805824 | bytes 6537216 | tf_op jit(solution)/shard_map/concatenate | solution.py:104
  13.4 1.7 copy-done.1
  15.8 1.3 reduce.39
  17.1 0.8 reshape.423
  17.9 7.6 %all-to-all-start = ((bf16[32,2,798]{2,1,0:T(2,128)(2,1)}), bf16[32,2,798]{2,1,0:T(2,128)(2,1)S(1)}, u32[]{:S(2)}, u32[]{:S(2)}) async-start(bf16[32,2,798]{2,1,0:T(2,128)(2,1)} %reshape.423), calls=%async_computation | async-start | bytes 229376 | tf_op jit(solution)/shard_map/all_to_all | solution.py:50
  25.5 4.3 %scatter_custom_fusion = s32[1024]{0:T(1024)S(1)} fusion(s32[1024]{0:T(1024)S(1)} %compare_select_fusion.1, s32[1024]{0:T(1024)S(1)} %iota.23, s32[]{:T(128)} %constant.75.clone.1), kind=kCustom, calls=%fused_computation.145 | custom fusion | bytes 4100 | tf_op jit(solution)/shard_map/scatter | solution.py:38
  37.1 0.8 reshape.425
  37.9 7.4 %all-to-all-start.1 = ((bf16[32,2,798]{2,1,0:T(2,128)(2,1)}), bf16[32,2,798]{2,1,0:T(2,128)(2,1)S(1)}, u32[]{:S(2)}, u32[]{:S(2)}) async-start(bf16[32,2,798]{2,1,0:T(2,128)(2,1)} %reshape.425), calls=%async_computation.1 | async-start | bytes 229376 | tf_op jit(solution)/shard_map/all_to_all | solution.py:53
  45.3 4.6 %gather_fusion.1 = bf16[32,399,128]{2,1,0:T(8,128)(2,1)} fusion(bf16[32,399,128]{2,1,0:T(8,128)(2,1)} %copy-done.1, s32[1024]{0:T(1024)S(1)} %pad_clamp_fusion.1), kind=kCustom, calls=%fused_computation.1 | custom fusion | bytes 6537344 | tf_op jit(solution)/shard_map/gather | solution.py:126
  49.9 1.3 all-to-all-done.1
  52.3 3.9 %broadcast_select_fusion = bf16[32,399,128]{2,1,0:T(8,128)(2,1)} fusion(bf16[32,399,128]{2,1,0:T(8,128)(2,1)} %gather_fusion.1, pred[32]{0:T(512)(128)(4,1)S(1)} %broadcast_compare_fusion.3, bf16[399,128]{1,0:T(8,128)(2,1)S(1)} %broadcast_in_dim.162), kind=kLoop, calls=%fused_computation.8 | loop fusion | flops 1634304 | bytes 6639392 | tf_op jit(solution)/shard_map/jit(_where)/select_n | solution.py:126
  56.2 6.5 %all-to-all-start.2 = ((bf16[32,399,128]{2,1,0:T(8,128)(2,1)}), bf16[32,399,128]{2,1,0:T(8,128)(2,1)}, u32[]{:S(2)}, u32[]{:S(2)}) async-start(bf16[32,399,128]{2,1,0:T(8,128)(2,1)} %broadcast_select_fusion), calls=%async_computation.2 | async-start | bytes 6553600 | tf_op jit(solution)/shard_map/all_to_all | solution.py:127
  62.9 28.9 %all_gather.3 = bf16[128,1536]{1,0:T(8,128)(2,1)S(1)} all-gather(bf16[16,1536]{1,0:T(8,128)(2,1)S(1)} %fusion.17), channel_id=1, replica_groups=mesh['req'=32,'head'=8] {'head'}, dimensions={0}, use_global_device_ids=true | all-gather | bytes 442368 | tf_op jit(solution)/shard_map/all_gather | solution.py:94
  92.5 2.2 %copy.278 = bf16[192,8,2,384]{3,1,2,0:T(8,128)(2,1)S(1)} copy(bf16[192,8,2,384]{3,2,1,0:T(2,128)(2,1)} %bitcast.74) | data formatting | bytes 4718592
  95.5 0.8 copy.238
  98.8 3.4 %all-to-all-done.2 = bf16[32,399,128]{2,1,0:T(8,128)(2,1)} async-done(((bf16[32,399,128]{2,1,0:T(8,128)(2,1)}), bf16[32,399,128]{2,1,0:T(8,128)(2,1)}, u32[]{:S(2)}, u32[]{:S(2)}) %all-to-all-start.2) | async-done | bytes 3268640 | tf_op jit(solution)/shard_map/all_to_all | solution.py:127
  102.2 4.6 %gather_fusion.2 = bf16[32,399,128]{2,1,0:T(8,128)(2,1)} fusion(bf16[32,399,128]{2,1,0:T(8,128)(2,1)} %all-to-all-done.2, s32[1024]{0:T(1024)S(1)} %pad_clamp_fusion), kind=kCustom, calls=%fused_computation.2 | custom fusion | bytes 6537344 | tf_op jit(solution)/shard_map/gather | solution.py:128
  106.8 4.0 %slice.275 = bf16[32,384,128]{2,1,0:T(8,128)(2,1)} slice(bf16[32,399,128]{2,1,0:T(8,128)(2,1)} %gather_fusion.2), slice={[0:32], [0:384], [0:128]} | slice | bytes 6291456 | tf_op jit(solution)/shard_map/slice | solution.py:129
  112.0 9.3 %fusion.45 = f32[32,4,6,64]{3,1,2,0:T(4,128)S(1)} fusion(bf16[32,6,64,128]{3,2,1,0:T(8,128)(2,1)} %bitcast.69, f32[32,4,256]{2,1,0:T(4,128)S(1)} %divide_multiply_fusion.1), kind=kOutput, calls=%fused_computation.93 | convolution fusion | flops 75497472 | bytes 3407872 | tf_op jit(solution)/shard_map/rhpn,rtn->rthp/dot_general | solution.py:164
  121.3 1.6 slice_reduce_fusion.9
  126.3 1.3 broadcast_multiply_fusion
  127.5 2.9 %fusion.32 = (f32[32,6,64]{2,1,0:T(8,128)S(1)}, f32[32,6,64]{2,1,0:T(8,128)S(1)}) fusion(f32[32,4,6,64]{3,1,2,0:T(4,128)S(1)} %get-tuple-element.62, f32[32,4,6,64]{3,1,2,0:T(4,128)S(1)} %fusion.45, f32[32]{0:T(128)} %get-tuple-element.40, f32[32,6]{1,0:T(8,128)} %bitcast.76, f32[6]{0:T(128)} %param.30, f32[32,4,6,64]{3,1,2,0:T(4,128)S(1)} %get-tuple-element.61, ...), kind=kLoop, calls=%fused_computation.79 | loop fusion | flops 196608 | bytes 495640 | tf_op jit(solution)/shard_map/add | solution.py:173
  133.6 2.4 %fusion.31 = (f32[32,6,64]{2,1,0:T(8,128)S(1)}, f32[32,6,64]{2,1,0:T(8,128)S(1)}) fusion(f32[32,4,6,64]{3,1,2,0:T(4,128)S(1)} %get-tuple-element.62, f32[32,4,6,64]{3,1,2,0:T(4,128)S(1)} %fusion.45, f32[32]{0:T(128)} %get-tuple-element.48, f32[32,6]{1,0:T(8,128)S(1)} %copy.244, f32[32,6]{1,0:T(8,128)S(1)} %copy.243, f32[6]{0:T(128)} %param.30, ...), kind=kLoop, calls=%fused_computation.78 | loop fusion | flops 196608 | bytes 446488 | tf_op jit(solution)/shard_map/add | solution.py:173
  136.3 1.0 select_convert_fusion
  138.2 1.0 pad_maximum_fusion.1
  141.2 13.4 %add_convert_fusion = bf16[32,6,64,128]{3,2,1,0:T(8,128)(2,1)} fusion(bf16[32,6,64,128]{3,2,1,0:T(8,128)(2,1)} %bitcast.70, f32[32,6]{1,0:T(8,128)S(1)} %copy-done.10, f32[32,4,6,64]{3,1,2,0:T(4,128)S(1)} %get-tuple-element.61, f32[32,4,6]{1,2,0:T(8,128)S(1)} %copy.259, f32[32,4,256]{2,1,0:T(4,128)S(1)} %divide_multiply_fusion.1), kind=kOutput, calls=%fused_computation.6 | convolution fusion | flops 81838080 | bytes 6897664 | tf_op jit(solution)/shard_map/rshp,rsn->rhpn/dot_general | solution.py:177
  154.6 24.7 %reduce-scatter.2.cloned.1.call-done = f32[16,1664]{1,0:T(8,128)} async-done(((f32[128,1664]{1,0:T(8,128)}), f32[16,1664]{1,0:T(8,128)}) %reduce-scatter.2.cloned.1.call-update) | async-done | bytes 106512 | tf_op jit(solution)/shard_map/reduce_scatter | solution.py:191
  179.3 0.9 fusion.56
  180.2 1.6 fusion.18
  (147 shorter events, 21.2 us)
Async XLA Ops:
  7.2 130.6 %copy-start = (bf16[384,1536]{1,0:T(8,128)(2,1)S(1)}, bf16[384,1536]{1,0:T(8,128)(2,1)}, u32[]{:S(2)}) copy-start(bf16[384,1536]{1,0:T(8,128)(2,1)} %param.32) | copy-start | bytes 3538948
  11.1 14.4 %copy-start.15 = (s32[1024]{0:T(1024)S(1)}, s32[1024]{0:T(1024)}, u32[]{:S(2)}) copy-start(s32[1024]{0:T(1024)} %param.39) | copy-start | bytes 12292
  11.1 19.8 %copy-start.23 = (s32[32]{0:T(128)S(1)}, s32[32]{0:T(128)}, u32[]{:S(2)}) copy-start(s32[32]{0:T(128)} %param.38) | copy-start | bytes 388
  11.1 22.4 %copy-start.8 = (bf16[16,1536]{1,0:T(8,128)(2,1)S(1)}, bf16[16,1536]{1,0:T(8,128)(2,1)}, u32[]{:S(2)}) copy-start(bf16[16,1536]{1,0:T(8,128)(2,1)} %param.20) | copy-start | bytes 147460
  13.4 1.7 copy-start.1
  17.9 17.7 %all-to-all-start = ((bf16[32,2,798]{2,1,0:T(2,128)(2,1)}), bf16[32,2,798]{2,1,0:T(2,128)(2,1)S(1)}, u32[]{:S(2)}, u32[]{:S(2)}) async-start(bf16[32,2,798]{2,1,0:T(2,128)(2,1)} %reshape.423), calls=%async_computation | async-start | bytes 229376 | tf_op jit(solution)/shard_map/all_to_all | solution.py:50
  37.9 13.3 %all-to-all-start.1 = ((bf16[32,2,798]{2,1,0:T(2,128)(2,1)}), bf16[32,2,798]{2,1,0:T(2,128)(2,1)S(1)}, u32[]{:S(2)}, u32[]{:S(2)}) async-start(bf16[32,2,798]{2,1,0:T(2,128)(2,1)} %reshape.425), calls=%async_computation.1 | async-start | bytes 229376 | tf_op jit(solution)/shard_map/all_to_all | solution.py:53
  56.2 6.6 %copy-start.13 = (f32[1536]{0:T(1024)S(1)}, f32[1536]{0:T(1024)}, u32[]{:S(2)}) copy-start(f32[1536]{0:T(1024)} %param.21) | copy-start | bytes 18436
  56.2 35.6 %copy-start.3 = (bf16[1536,304]{0,1:T(8,128)(2,1)S(1)}, bf16[1536,304]{0,1:T(8,128)(2,1)}, u32[]{:S(2)}) copy-start(bf16[1536,304]{0,1:T(8,128)(2,1)} %param.23) | copy-start | bytes 2801668
  56.2 45.9 %all-to-all-start.2 = ((bf16[32,399,128]{2,1,0:T(8,128)(2,1)}), bf16[32,399,128]{2,1,0:T(8,128)(2,1)}, u32[]{:S(2)}, u32[]{:S(2)}) async-start(bf16[32,399,128]{2,1,0:T(8,128)(2,1)} %broadcast_select_fusion), calls=%async_computation.2 | async-start | bytes 6553600 | tf_op jit(solution)/shard_map/all_to_all | solution.py:127
  62.7 116.6 %reduce-scatter.2.cloned.1.call-start = ((), (), s32[]{:S(2)}) async-start(), calls=%async_computation.4 | async-start | bytes 958464 | tf_op jit(solution)/shard_map/reduce_scatter | solution.py:191
  92.4 3.0 %copy-start.21 = (s32[32]{0:T(128)S(1)}, s32[32]{0:T(128)}, u32[]{:S(2)}) copy-start(s32[32]{0:T(128)} %param.36) | copy-start | bytes 388
  92.4 3.0 %copy-start.24 = (f32[6]{0:T(128)S(1)}, f32[6]{0:T(128)}, u32[]{:S(2)}) copy-start(f32[6]{0:T(128)} %param.29) | copy-start | bytes 76
  92.4 3.0 %copy-start.20 = (f32[6]{0:T(128)S(1)}, f32[6]{0:T(128)}, u32[]{:S(2)}) copy-start(f32[6]{0:T(128)} %param.28) | copy-start | bytes 76
  92.4 5.5 %copy-start.14 = (f32[4,384]{1,0:T(4,128)S(1)}, f32[4,384]{1,0:T(4,128)}, u32[]{:S(2)}) copy-start(f32[4,384]{1,0:T(4,128)} %param.24) | copy-start | bytes 18436
  92.5 5.6 %copy-start.16 = (f32[4,256]{1,0:T(4,128)S(1)}, f32[4,256]{1,0:T(4,128)}, u32[]{:S(2)}) copy-start(f32[4,256]{1,0:T(4,128)} %param.26) | copy-start | bytes 12292
  95.4 11.4 %copy-start.18 = (pred[32,4]{0,1:T(4,128)(4,1)}, pred[32,4]{0,1:T(4,128)(4,1)S(1)}, u32[]{:S(2)}) copy-start(pred[32,4]{0,1:T(4,128)(4,1)S(1)} %iota_compare_fusion.1) | copy-start | bytes 388
  106.8 4.1 %copy-start.2 = (bf16[32,399,128]{2,1,0:T(8,128)(2,1)S(1)}, bf16[32,399,128]{2,1,0:T(8,128)(2,1)}, u32[]{:S(2)}) copy-start(bf16[32,399,128]{2,1,0:T(8,128)(2,1)} %gather_fusion.2) | copy-start | bytes 9805828
  106.8 4.1 %slice-start = ((bf16[32,399,128]{2,1,0:T(8,128)(2,1)}), bf16[32,9,128]{2,1,0:T(8,128)(2,1)S(1)}, s32[]{:S(2)}) async-start(bf16[32,399,128]{2,1,0:T(8,128)(2,1)} %gather_fusion.2), calls=%async_computation.5 | async-start | bytes 262144 | tf_op jit(solution)/shard_map/slice | solution.py:130
  106.8 4.3 %copy-start.17 = (f32[384]{0:T(512)S(1)}, f32[384]{0:T(512)}, u32[]{:S(2)}) copy-start(f32[384]{0:T(512)} %param.25) | copy-start | bytes 4612
  110.8 0.7 copy-start.19
  110.9 10.4 %copy-start.4 = (bf16[32,3,384]{2,1,0:T(4,128)(2,1)}, bf16[32,3,384]{2,1,0:T(4,128)(2,1)S(1)}, u32[]{:S(2)}) copy-start(bf16[32,3,384]{2,1,0:T(4,128)(2,1)S(1)} %reshape.335) | copy-start | bytes 221188
  111.3 14.3 %copy-start.6 = (bf16[32,3,256]{2,1,0:T(4,128)(2,1)}, bf16[32,3,256]{2,1,0:T(4,128)(2,1)S(1)}, u32[]{:S(2)}) copy-start(bf16[32,3,256]{2,1,0:T(4,128)(2,1)S(1)} %reshape.333) | copy-start | bytes 147460
  136.0 3.3 %copy-start.11 = (f32[32,1,6]{0,1,2:T(1,128)S(1)}, f32[32,1,6]{0,1,2:T(1,128)}, u32[]{:S(2)}) copy-start(f32[32,1,6]{0,1,2:T(1,128)} %get-tuple-element.54) | copy-start | bytes 2308
  136.0 3.3 %copy-start.12 = (f32[32,1,6]{0,1,2:T(1,128)S(1)}, f32[32,1,6]{0,1,2:T(1,128)}, u32[]{:S(2)}) copy-start(f32[32,1,6]{0,1,2:T(1,128)} %get-tuple-element.55) | copy-start | bytes 2308
  136.0 3.5 %copy-start.22 = (s32[32]{0:T(128)S(1)}, s32[32]{0:T(128)}, u32[]{:S(2)}) copy-start(s32[32]{0:T(128)} %param.36) | copy-start | bytes 388
  136.3 3.3 %copy-start.7 = (bf16[32,3,256]{2,1,0:T(4,128)(2,1)S(1)}, bf16[32,3,256]{2,1,0:T(4,128)(2,1)}, u32[]{:S(2)}) copy-start(bf16[32,3,256]{2,1,0:T(4,128)(2,1)} %copy-done.6) | copy-start | bytes 147460
  137.3 3.2 %copy-start.5 = (bf16[32,3,384]{2,1,0:T(4,128)(2,1)S(1)}, bf16[32,3,384]{2,1,0:T(4,128)(2,1)}, u32[]{:S(2)}) copy-start(bf16[32,3,384]{2,1,0:T(4,128)(2,1)} %copy-done.4) | copy-start | bytes 221188
  137.6 3.6 %copy-start.10 = (f32[32,6]{1,0:T(8,128)S(1)}, f32[32,6]{1,0:T(8,128)}, u32[]{:S(2)}) copy-start(f32[32,6]{1,0:T(8,128)} %copy.250) | copy-start | bytes 2308
  141.2 39.0 %copy-start.9 = (bf16[16,1536]{1,0:T(8,128)(2,1)S(1)}, bf16[16,1536]{1,0:T(8,128)(2,1)}, u32[]{:S(2)}) copy-start(bf16[16,1536]{1,0:T(8,128)(2,1)} %param.20) | copy-start | bytes 147460
Sparse Core Ops, SparseCore 0:
  139.3 39.9 reduce-scatter.1
where the time goes:
time: 190 us; the launch traced here: 189 us
  local copies, waits for them, and re-layouts  42.9 us (23%)
  waiting for transfers between devices  29.5 us (16%)
  blocking collectives  28.9 us (15%)
  matrix products  24.2 us (13%)
  other arithmetic  23.6 us (12%)
  starting transfers between devices  21.5 us (11%)
  between operations  18 us (9%)
    all_gather x1, blocking collectives, local(): piece_rows = lax.all_gather(normed, 'head', axis=0, tiled=True)  28.9 us
    reduce_scatter x1, waiting for transfers between devices, local(): lax.psum_scatter(combined, 'head', scatter_dimension=0, tiled=True)  24.7 us
    dot_general x1, matrix products, local(): update = jnp.einsum('rshp,rsn->rhpn', pushed, entries, precision=HIGH)  13.4 us
    dot_general x1, matrix products, local(): from_state = jnp.einsum('rhpn,rtn->rthp', held, readouts, precision=HIGH)  9.26 us
    unnamed x61, local copies, waits for them, and re-layouts  8.57 us
    all_to_all x1, starting transfers between devices, migrate(): first = lax.all_to_all(padded, 'req', 0, 0, tiled=True)  7.56 us
    all_to_all x1, starting transfers between devices, migrate(): second = lax.all_to_all(first[order], 'req', 0, 0, tiled=True)  7.38 us
    all_to_all x1, starting transfers between devices, local(): received = lax.all_to_all(send_buf, 'req', 0, 0, tiled=True)  6.51 us
  transfers between devices with their start and end apart: 4, of which 3 were waited for; matrix products, arithmetic and copies ran while one was open for 18% of the time, Pallas kernels for 0%

commit v1 on v0

--- a/solution.py
+++ b/solution.py
@@ -91,7 +91,8 @@
         rows_in * lax.rsqrt(jnp.mean(rows_in * rows_in, axis=-1, keepdims=True) + EPS) * pre_gain
     ).astype(jnp.bfloat16)
     inner_flat = inner_weight.reshape(inner_weight.shape[0], 2 * inner_here)
-    piece_rows = lax.all_gather(normed, "head", axis=0, tiled=True)
+    sent = jnp.stack([normed] * lax.axis_size("head"))
+    piece_rows = jnp.concatenate(lax.all_to_all(sent, "head", 0, 0), axis=0)
     inner_rows = jnp.dot(piece_rows, inner_flat, preferred_element_type=jnp.float32).astype(
         jnp.bfloat16
     )

time: 190 us -> 202 us (1.063)
  blocking collectives: 28.9 us -> 0 us
  waiting for transfers between devices: 29.5 us -> 44.1 us
  local copies, waits for them, and re-layouts: 42.9 us -> 54 us
  starting transfers between devices: 21.5 us -> 30 us
  matrix products: 24.2 us -> 27.8 us
  other arithmetic: 23.6 us -> 26.2 us
    all_gather x1 -> x0, blocking collectives: 28.9 us -> none  [local(): piece_rows = lax.all_gather(normed, 'head', axis=0, tiled=True)]
    all_to_all x1, waiting for transfers between devices: 3.41 us -> 16.7 us  [local(): received = lax.all_to_all(send_buf, 'req', 0, 0, tiled=True)]
    all_to_all x0 -> x1, starting transfers between devices: none -> 8.47 us  [local(): piece_rows = jnp.concatenate(lax.all_to_all(sent, 'head', 0, 0), axis=0)]
    reduce_scatter x1, waiting for transfers between devices: 24.7 us -> 19.9 us  [local(): lax.psum_scatter(combined, 'head', scatter_dimension=0, tiled=True)]
    all_to_all x0 -> x1, waiting for transfers between devices: none -> 3.56 us  [local(): piece_rows = jnp.concatenate(lax.all_to_all(sent, 'head', 0, 0), axis=0)]
    all_to_all x1, waiting for transfers between devices: 1.33 us -> 3.97 us  [migrate(): second = lax.all_to_all(first[order], 'req', 0, 0, tiled=True)]
    unnamed x61 -> x67, local copies, waits for them, and re-layouts: 8.57 us -> 9.29 us
  transfers between devices with their start and end apart: 4 -> 5, of which waited for: 3 -> 4; matrix products, arithmetic and copies ran while one was open for 18% -> 27% of each run, Pallas kernels for 0% -> 0%
where the time goes in v1:
time: 202 us; the launch traced here: 200 us
  local copies, waits for them, and re-layouts  54 us (27%)
  waiting for transfers between devices  44.1 us (22%)
  starting transfers between devices  30 us (15%)
  matrix products  27.8 us (14%)
  other arithmetic  26.2 us (13%)
  between operations  17.9 us (9%)
    reduce_scatter x1, waiting for transfers between devices, local(): lax.psum_scatter(combined, 'head', scatter_dimension=0, tiled=True)  19.9 us
    all_to_all x1, waiting for transfers between devices, local(): received = lax.all_to_all(send_buf, 'req', 0, 0, tiled=True)  16.7 us
    dot_general x1, matrix products, local(): update = jnp.einsum('rshp,rsn->rhpn', pushed, entries, precision=HIGH)  13.4 us
    unnamed x67, local copies, waits for them, and re-layouts  9.29 us
    dot_general x1, matrix products, local(): from_state = jnp.einsum('rhpn,rtn->rthp', held, readouts, precision=HIGH)  9.26 us
    all_to_all x1, starting transfers between devices, local(): piece_rows = jnp.concatenate(lax.all_to_all(sent, 'head', 0, 0), axis=0)  8.47 us
    all_to_all x1, starting transfers between devices, migrate(): first = lax.all_to_all(padded, 'req', 0, 0, tiled=True)  7.56 us
    all_to_all x1, starting transfers between devices, migrate(): second = lax.all_to_all(first[order], 'req', 0, 0, tiled=True)  7.38 us
  transfers between devices with their start and end apart: 5, of which 4 were waited for; matrix products, arithmetic and copies ran while one was open for 27% of the time, Pallas kernels for 0%

profile of v1, /device:TPU:6, one launch (start us, length us, event | category | flops | bytes accessed | tf_op | source)
XLA Modules:
  0.0 200.1 jit_solution(9827122690681241946)
XLA Ops:
  7.2 1.3 dynamic_slice.26
  11.1 2.3 %pad_maximum_fusion = bf16[32,399,128]{2,1,0:T(8,128)(2,1)S(1)} fusion(bf16[32,6,128]{2,1,0:T(8,128)(2,1)S(1)} %reshape.338, bf16[32,9,128]{2,1,0:T(8,128)(2,1)S(1)} %reshape.337, bf16[32,384,128]{2,1,0:T(8,128)(2,1)} %bitcast.76), kind=kLoop, calls=%fused_computation.7 | loop fusion | flops 9805824 | bytes 6537216 | tf_op jit(solution)/shard_map/concatenate | solution.py:105
  13.4 1.7 copy-done.1
  15.8 1.3 reduce.39
  17.9 7.6 %all-to-all-start.1 = ((bf16[32,2,798]{2,1,0:T(2,128)(2,1)}), bf16[32,2,798]{2,1,0:T(2,128)(2,1)S(1)}, u32[]{:S(2)}, u32[]{:S(2)}) async-start(bf16[32,2,798]{2,1,0:T(2,128)(2,1)} %reshape.429), calls=%async_computation.1 | async-start | bytes 229376 | tf_op jit(solution)/shard_map/all_to_all | solution.py:50
  25.7 4.3 %scatter_custom_fusion = s32[1024]{0:T(1024)S(1)} fusion(s32[1024]{0:T(1024)S(1)} %compare_select_fusion.1, s32[1024]{0:T(1024)S(1)} %iota.23, s32[]{:T(128)} %constant.75.clone.1), kind=kCustom, calls=%fused_computation.145 | custom fusion | bytes 4100 | tf_op jit(solution)/shard_map/scatter | solution.py:38
  34.2 7.4 %all-to-all-start.2 = ((bf16[32,2,798]{2,1,0:T(2,128)(2,1)}), bf16[32,2,798]{2,1,0:T(2,128)(2,1)S(1)}, u32[]{:S(2)}, u32[]{:S(2)}) async-start(bf16[32,2,798]{2,1,0:T(2,128)(2,1)} %reshape.431), calls=%async_computation.2 | async-start | bytes 229376 | tf_op jit(solution)/shard_map/all_to_all | solution.py:53
  43.5 4.0 %all-to-all-done.2 = bf16[32,2,798]{2,1,0:T(2,128)(2,1)S(1)} async-done(((bf16[32,2,798]{2,1,0:T(2,128)(2,1)}), bf16[32,2,798]{2,1,0:T(2,128)(2,1)S(1)}, u32[]{:S(2)}, u32[]{:S(2)}) %all-to-all-start.2) | async-done | bytes 102176 | tf_op jit(solution)/shard_map/all_to_all | solution.py:53
  48.3 8.5 %all-to-all-start = ((bf16[8,16,1536]{2,1,0:T(8,128)(2,1)}), bf16[8,16,1536]{2,1,0:T(8,128)(2,1)S(1)}, u32[]{:S(2)}, u32[]{:S(2)}) async-start(bf16[8,16,1536]{2,1,0:T(8,128)(2,1)} %stack.14), calls=%async_computation | async-start | bytes 786432 | tf_op jit(solution)/shard_map/all_to_all | solution.py:95
  56.8 4.6 %gather_fusion.1 = bf16[32,399,128]{2,1,0:T(8,128)(2,1)} fusion(bf16[32,399,128]{2,1,0:T(8,128)(2,1)} %copy-done.1, s32[1024]{0:T(1024)S(1)} %pad_clamp_fusion.1), kind=kCustom, calls=%fused_computation.1 | custom fusion | bytes 6537344 | tf_op jit(solution)/shard_map/gather | solution.py:127
  64.2 3.9 %broadcast_select_fusion = bf16[32,399,128]{2,1,0:T(8,128)(2,1)} fusion(bf16[32,399,128]{2,1,0:T(8,128)(2,1)} %gather_fusion.1, pred[32]{0:T(512)(128)(4,1)S(1)} %broadcast_compare_fusion.3, bf16[399,128]{1,0:T(8,128)(2,1)S(1)} %broadcast_in_dim.162), kind=kLoop, calls=%fused_computation.8 | loop fusion | flops 1634304 | bytes 6639392 | tf_op jit(solution)/shard_map/jit(_where)/select_n | solution.py:127
  68.1 3.6 %all-to-all-done = bf16[8,16,1536]{2,1,0:T(8,128)(2,1)S(1)} async-done(((bf16[8,16,1536]{2,1,0:T(8,128)(2,1)}), bf16[8,16,1536]{2,1,0:T(8,128)(2,1)S(1)}, u32[]{:S(2)}, u32[]{:S(2)}) %all-to-all-start) | async-done | bytes 393248 | tf_op jit(solution)/shard_map/all_to_all | solution.py:95
  72.4 6.4 %all-to-all-start.3 = ((bf16[32,399,128]{2,1,0:T(8,128)(2,1)}), bf16[32,399,128]{2,1,0:T(8,128)(2,1)}, u32[]{:S(2)}, u32[]{:S(2)}) async-start(bf16[32,399,128]{2,1,0:T(8,128)(2,1)} %broadcast_select_fusion), calls=%async_computation.3 | async-start | bytes 6553600 | tf_op jit(solution)/shard_map/all_to_all | solution.py:128
  79.1 2.1 %copy.278 = bf16[192,8,2,384]{3,1,2,0:T(8,128)(2,1)S(1)} copy(bf16[192,8,2,384]{3,2,1,0:T(2,128)(2,1)} %bitcast.77) | data formatting | bytes 4718592
  84.2 1.4 fusion.72
  85.6 2.3 %convolution_convert_fusion.1 = bf16[128,304]{0,1:T(8,128)(2,1)} fusion(bf16[128,1536]{1,0:T(8,128)(2,1)} %bitcast.74, bf16[1536,304]{0,1:T(8,128)(2,1)} %param.23), kind=kOutput, calls=%fused_computation.10 | convolution fusion | flops 119576576 | bytes 1404928 | tf_op jit(solution)/shard_map/dot_general | solution.py:99
  87.9 1.6 copy.230
  89.5 1.6 reshape.335
  91.1 1.4 slice.266
  92.5 1.5 slice.269
  94.0 2.1 %convolution_convert_fusion = bf16[128,768]{1,0:T(8,128)(2,1)} fusion(bf16[128,1536]{1,0:T(8,128)(2,1)} %bitcast.75, bf16[1536,768]{1,0:T(8,128)(2,1)S(1)} %bitcast.72), kind=kOutput, calls=%fused_computation.9 | convolution fusion | flops 302088192 | bytes 2949120 | tf_op jit(solution)/shard_map/dot_general | solution.py:96
  101.6 16.7 %all-to-all-done.3 = bf16[32,399,128]{2,1,0:T(8,128)(2,1)} async-done(((bf16[32,399,128]{2,1,0:T(8,128)(2,1)}), bf16[32,399,128]{2,1,0:T(8,128)(2,1)}, u32[]{:S(2)}, u32[]{:S(2)}) %all-to-all-start.3) | async-done | bytes 3268640 | tf_op jit(solution)/shard_map/all_to_all | solution.py:128
  118.3 4.7 %gather_fusion.2 = bf16[32,399,128]{2,1,0:T(8,128)(2,1)} fusion(bf16[32,399,128]{2,1,0:T(8,128)(2,1)} %all-to-all-done.3, s32[1024]{0:T(1024)} %pad_clamp_fusion), kind=kCustom, calls=%fused_computation.2 | custom fusion | bytes 6537344 | tf_op jit(solution)/shard_map/gather | solution.py:129
  123.0 4.0 %slice.275 = bf16[32,384,128]{2,1,0:T(8,128)(2,1)} slice(bf16[32,399,128]{2,1,0:T(8,128)(2,1)} %gather_fusion.2), slice={[0:32], [0:384], [0:128]} | slice | bytes 6291456 | tf_op jit(solution)/shard_map/slice | solution.py:130
  128.3 9.3 %fusion.45 = f32[32,4,6,64]{3,1,2,0:T(4,128)S(1)} fusion(bf16[32,6,64,128]{3,2,1,0:T(8,128)(2,1)} %bitcast.70, f32[32,4,256]{2,1,0:T(4,128)S(1)} %divide_multiply_fusion.1), kind=kOutput, calls=%fused_computation.93 | convolution fusion | flops 75497472 | bytes 3407872 | tf_op jit(solution)/shard_map/rhpn,rtn->rthp/dot_general | solution.py:165
  137.6 1.6 slice_reduce_fusion.9
  142.5 1.3 broadcast_multiply_fusion
  143.8 2.9 %fusion.32 = (f32[32,6,64]{2,1,0:T(8,128)S(1)}, f32[32,6,64]{2,1,0:T(8,128)S(1)}) fusion(f32[32,4,6,64]{3,1,2,0:T(4,128)S(1)} %get-tuple-element.62, f32[32,4,6,64]{3,1,2,0:T(4,128)S(1)} %fusion.45, f32[32]{0:T(128)} %get-tuple-element.40, f32[32,6]{1,0:T(8,128)} %bitcast.79, f32[6]{0:T(128)} %param.30, f32[32,4,6,64]{3,1,2,0:T(4,128)S(1)} %get-tuple-element.61, ...), kind=kLoop, calls=%fused_computation.79 | loop fusion | flops 196608 | bytes 495640 | tf_op jit(solution)/shard_map/add | solution.py:174
  149.9 2.4 %fusion.31 = (f32[32,6,64]{2,1,0:T(8,128)S(1)}, f32[32,6,64]{2,1,0:T(8,128)S(1)}) fusion(f32[32,4,6,64]{3,1,2,0:T(4,128)S(1)} %get-tuple-element.62, f32[32,4,6,64]{3,1,2,0:T(4,128)S(1)} %fusion.45, f32[32]{0:T(128)} %get-tuple-element.48, f32[32,6]{1,0:T(8,128)S(1)} %copy.244, f32[32,6]{1,0:T(8,128)S(1)} %copy.243, f32[6]{0:T(128)} %param.30, ...), kind=kLoop, calls=%fused_computation.78 | loop fusion | flops 196608 | bytes 446488 | tf_op jit(solution)/shard_map/add | solution.py:174
  157.5 13.4 %add_convert_fusion = bf16[32,6,64,128]{3,2,1,0:T(8,128)(2,1)} fusion(bf16[32,6,64,128]{3,2,1,0:T(8,128)(2,1)} %bitcast.71, f32[32,6]{1,0:T(8,128)S(1)} %copy-done.10, f32[32,4,6,64]{3,1,2,0:T(4,128)S(1)} %get-tuple-element.61, f32[32,4,6]{1,2,0:T(8,128)S(1)} %copy.259, f32[32,4,256]{2,1,0:T(4,128)S(1)} %divide_multiply_fusion.1), kind=kOutput, calls=%fused_computation.6 | convolution fusion | flops 81838080 | bytes 6897664 | tf_op jit(solution)/shard_map/rshp,rsn->rhpn/dot_general | solution.py:178
  170.9 19.9 %reduce-scatter.2.cloned.1.call-done = f32[16,1664]{1,0:T(8,128)} async-done(((f32[128,1664]{1,0:T(8,128)}), f32[16,1664]{1,0:T(8,128)}) %reduce-scatter.2.cloned.1.call-update) | async-done | bytes 106512 | tf_op jit(solution)/shard_map/reduce_scatter | solution.py:192
  191.6 1.6 fusion.18
  (155 shorter events, 33.7 us)
Async XLA Ops:
  7.2 146.8 %copy-start = (bf16[384,1536]{1,0:T(8,128)(2,1)S(1)}, bf16[384,1536]{1,0:T(8,128)(2,1)}, u32[]{:S(2)}) copy-start(bf16[384,1536]{1,0:T(8,128)(2,1)} %param.32) | copy-start | bytes 3538948
  11.1 14.4 %copy-start.8 = (bf16[16,1536]{1,0:T(8,128)(2,1)S(1)}, bf16[16,1536]{1,0:T(8,128)(2,1)}, u32[]{:S(2)}) copy-start(bf16[16,1536]{1,0:T(8,128)(2,1)} %param.20) | copy-start | bytes 147460
  11.1 14.6 %copy-start.18 = (s32[1024]{0:T(1024)S(1)}, s32[1024]{0:T(1024)}, u32[]{:S(2)}) copy-start(s32[1024]{0:T(1024)} %param.39) | copy-start | bytes 12292
  11.1 19.9 %copy-start.27 = (s32[32]{0:T(128)S(1)}, s32[32]{0:T(128)}, u32[]{:S(2)}) copy-start(s32[32]{0:T(128)} %param.38) | copy-start | bytes 388
  13.4 1.7 copy-start.1
  15.1 26.4 %copy-start.16 = (f32[1536]{0:T(1024)S(1)}, f32[1536]{0:T(1024)}, u32[]{:S(2)}) copy-start(f32[1536]{0:T(1024)} %param.21) | copy-start | bytes 18436
  17.9 13.9 %all-to-all-start.1 = ((bf16[32,2,798]{2,1,0:T(2,128)(2,1)}), bf16[32,2,798]{2,1,0:T(2,128)(2,1)S(1)}, u32[]{:S(2)}, u32[]{:S(2)}) async-start(bf16[32,2,798]{2,1,0:T(2,128)(2,1)} %reshape.429), calls=%async_computation.1 | async-start | bytes 229376 | tf_op jit(solution)/shard_map/all_to_all | solution.py:50
  34.2 13.3 %all-to-all-start.2 = ((bf16[32,2,798]{2,1,0:T(2,128)(2,1)}), bf16[32,2,798]{2,1,0:T(2,128)(2,1)S(1)}, u32[]{:S(2)}, u32[]{:S(2)}) async-start(bf16[32,2,798]{2,1,0:T(2,128)(2,1)} %reshape.431), calls=%async_computation.2 | async-start | bytes 229376 | tf_op jit(solution)/shard_map/all_to_all | solution.py:53
  48.3 23.4 %all-to-all-start = ((bf16[8,16,1536]{2,1,0:T(8,128)(2,1)}), bf16[8,16,1536]{2,1,0:T(8,128)(2,1)S(1)}, u32[]{:S(2)}, u32[]{:S(2)}) async-start(bf16[8,16,1536]{2,1,0:T(8,128)(2,1)} %stack.14), calls=%async_computation | async-start | bytes 786432 | tf_op jit(solution)/shard_map/all_to_all | solution.py:95
  71.7 0.7 copy-start.3
  72.4 45.8 %all-to-all-start.3 = ((bf16[32,399,128]{2,1,0:T(8,128)(2,1)}), bf16[32,399,128]{2,1,0:T(8,128)(2,1)}, u32[]{:S(2)}, u32[]{:S(2)}) async-start(bf16[32,399,128]{2,1,0:T(8,128)(2,1)} %broadcast_select_fusion), calls=%async_computation.3 | async-start | bytes 6553600 | tf_op jit(solution)/shard_map/all_to_all | solution.py:128
  78.9 3.4 %copy-start.17 = (f32[4,384]{1,0:T(4,128)S(1)}, f32[4,384]{1,0:T(4,128)}, u32[]{:S(2)}) copy-start(f32[4,384]{1,0:T(4,128)} %param.24) | copy-start | bytes 18436
  78.9 111.9 %reduce-scatter.2.cloned.1.call-start = ((), (), s32[]{:S(2)}) async-start(), calls=%async_computation.5 | async-start | bytes 958464 | tf_op jit(solution)/shard_map/reduce_scatter | solution.py:192
  83.5 39.5 %copy-start.24 = (pred[32,4]{0,1:T(4,128)(4,1)}, pred[32,4]{0,1:T(4,128)(4,1)S(1)}, u32[]{:S(2)}) copy-start(pred[32,4]{0,1:T(4,128)(4,1)S(1)} %iota_compare_fusion.1) | copy-start | bytes 388
  123.0 4.1 %copy-start.2 = (bf16[32,399,128]{2,1,0:T(8,128)(2,1)S(1)}, bf16[32,399,128]{2,1,0:T(8,128)(2,1)}, u32[]{:S(2)}) copy-start(bf16[32,399,128]{2,1,0:T(8,128)(2,1)} %gather_fusion.2) | copy-start | bytes 9805828
  123.0 4.2 %slice-start = ((bf16[32,399,128]{2,1,0:T(8,128)(2,1)}), bf16[32,9,128]{2,1,0:T(8,128)(2,1)S(1)}, s32[]{:S(2)}) async-start(bf16[32,399,128]{2,1,0:T(8,128)(2,1)} %gather_fusion.2), calls=%async_computation.6 | async-start | bytes 262144 | tf_op jit(solution)/shard_map/slice | solution.py:131
  123.0 4.3 %copy-start.13 = (f32[384]{0:T(512)S(1)}, f32[384]{0:T(512)}, u32[]{:S(2)}) copy-start(f32[384]{0:T(512)} %get-tuple-element.51) | copy-start | bytes 4612
  123.0 4.3 %copy-start.14 = (f32[384]{0:T(512)S(1)}, f32[384]{0:T(512)}, u32[]{:S(2)}) copy-start(f32[384]{0:T(512)} %get-tuple-element.52) | copy-start | bytes 4612
  123.0 4.3 %copy-start.15 = (f32[384]{0:T(512)S(1)}, f32[384]{0:T(512)}, u32[]{:S(2)}) copy-start(f32[384]{0:T(512)} %get-tuple-element.53) | copy-start | bytes 4612
  123.0 4.3 %copy-start.23 = (f32[384]{0:T(512)S(1)}, f32[384]{0:T(512)}, u32[]{:S(2)}) copy-start(f32[384]{0:T(512)} %param.25) | copy-start | bytes 4612
  123.0 4.6 %copy-start.5 = (bf16[32,4,256]{2,1,0:T(4,128)(2,1)S(1)}, bf16[32,4,256]{2,1,0:T(4,128)(2,1)}, u32[]{:S(2)}) copy-start(bf16[32,4,256]{2,1,0:T(4,128)(2,1)} %slice.269) | copy-start | bytes 196612
  127.1 0.7 copy-start.20
  127.1 0.7 copy-start.21
  127.1 0.7 copy-start.25
  127.6 14.2 %copy-start.6 = (bf16[32,3,256]{2,1,0:T(4,128)(2,1)}, bf16[32,3,256]{2,1,0:T(4,128)(2,1)S(1)}, u32[]{:S(2)}) copy-start(bf16[32,3,256]{2,1,0:T(4,128)(2,1)S(1)} %reshape.339) | copy-start | bytes 147460
  152.3 3.3 %copy-start.26 = (s32[32]{0:T(128)S(1)}, s32[32]{0:T(128)}, u32[]{:S(2)}) copy-start(s32[32]{0:T(128)} %param.36) | copy-start | bytes 388
  152.3 3.3 %copy-start.11 = (f32[32,1,6]{0,1,2:T(1,128)S(1)}, f32[32,1,6]{0,1,2:T(1,128)}, u32[]{:S(2)}) copy-start(f32[32,1,6]{0,1,2:T(1,128)} %get-tuple-element.54) | copy-start | bytes 2308
  152.3 3.2 %copy-start.12 = (f32[32,1,6]{0,1,2:T(1,128)S(1)}, f32[32,1,6]{0,1,2:T(1,128)}, u32[]{:S(2)}) copy-start(f32[32,1,6]{0,1,2:T(1,128)} %get-tuple-element.55) | copy-start | bytes 2308
  152.5 3.3 %copy-start.4 = (bf16[32,4,304]{2,1,0:T(4,128)(2,1)S(1)}, bf16[32,4,304]{2,1,0:T(4,128)(2,1)}, u32[]{:S(2)}) copy-start(bf16[32,4,304]{2,1,0:T(4,128)(2,1)} %reshape.335) | copy-start | bytes 233476
  152.5 3.3 %copy-start.7 = (bf16[32,3,256]{2,1,0:T(4,128)(2,1)S(1)}, bf16[32,3,256]{2,1,0:T(4,128)(2,1)}, u32[]{:S(2)}) copy-start(bf16[32,3,256]{2,1,0:T(4,128)(2,1)} %copy-done.6) | copy-start | bytes 147460
  153.9 3.6 %copy-start.10 = (f32[32,6]{1,0:T(8,128)S(1)}, f32[32,6]{1,0:T(8,128)}, u32[]{:S(2)}) copy-start(f32[32,6]{1,0:T(8,128)} %copy.250) | copy-start | bytes 2308
  157.5 34.1 %copy-start.9 = (bf16[16,1536]{1,0:T(8,128)(2,1)S(1)}, bf16[16,1536]{1,0:T(8,128)(2,1)}, u32[]{:S(2)}) copy-start(bf16[16,1536]{1,0:T(8,128)(2,1)} %param.20) | copy-start | bytes 147460
  (2 other events, 1.3 us)
Sparse Core Ops, SparseCore 0:
  155.6 35.1 reduce-scatter.1
